TPU v7x, 256 devices: a whole 4x4x8 slice. The times are simulated.
256 devices in a mesh: gx: 8 (over z_hi, core), gy: 8 (over z_lo, y), gz: 4 (over x).
Axes of the slice: x: 4, y: 4, z: 8 (z_hi: 4, z_lo: 2; z = z_hi * 2 + z_lo), core: 2. Of those that a mesh axis runs over, the one named last changes fastest.
Arguments:
- blocks: bfloat16 [16, 8, 8, 27, 128, 128], P('gx', 'gy', 'gz')
- pattern: int32 [16, 8, 8, 27], P('gx', 'gy'), may hold values 0 or 1
- order: int32 [16, 8, 8], P('gx', 'gy'), may hold values from 0 to 7, each once within a row
- start: float32 [16, 8, 8, 128], P('gx', 'gy', 'gz'), may hold values from -6 to 6
- rhs: float32 [16, 8, 8, 128], P('gx', 'gy', 'gz'), may hold values from -6 to 6
Outputs:
- smoothed: float32 [16, 8, 8, 128], P('gx', 'gy', 'gz')
- remainder: float32 [16, 8, 8, 128], P('gx', 'gy', 'gz')
Inputs may be any that keep to these rules, and one draw needn't show every extreme that they name: `order`: in every grid column the 8 slots name each plane exactly once. `pattern`: entry 13 is ignored.
All inputs are finite; a program needn't handle non-finite values. No bound on the sum of `pattern` on one device may be relied on, other than what follows from the above.
Results may differ from a plain program's by a relative error of at most 0.0081.
Values may be sent and summed in bfloat16 or wider, within the bound.
A program may use at most 64 MiB of HBM per device.

v0:
```python
import jax
import jax.numpy as jnp
from jax import lax
from jax.sharding import PartitionSpec as P

DEG = 4


def padded_2(cells, sides, width):
    for axis, dim in sides:
        count = lax.axis_size(axis)
        ends = count - 1
        head = lax.slice_in_dim(cells, 0, width, axis=dim)
        tail = lax.slice_in_dim(cells, cells.shape[dim] - width, cells.shape[dim], axis=dim)
        cells = jnp.concatenate(
            [
                lax.ppermute(tail, axis, [(i, (i + 1) % count) for i in range(ends)]),
                cells,
                lax.ppermute(head, axis, [((i + 1) % count, i) for i in range(ends)]),
            ],
            axis=dim,
        )
    return cells


def coupled_product(matrix, planes, rows, present):
    padded = padded_2(planes, (("gx", 0), ("gy", 1)), 1)
    padded = jnp.pad(padded, ((0, 0), (0, 0), (1, 1), (0, 0)))
    span_x, span_y = (planes.shape[0], planes.shape[1])
    height = padded.shape[2]
    keeping = jnp.where(jnp.arange(27) == 13, 1, present).astype(jnp.float32)
    offsets = jnp.arange(3, dtype=jnp.int32)
    places = jnp.arange(height, dtype=jnp.int32)
    target = rows[..., None, None] + offsets[:, None]
    select = (target == places).astype(jnp.float32)
    pieces = []
    for step_a in range(3):
        for step_b in range(3):
            column = padded[step_a : step_a + span_x, step_b : step_b + span_y]
            first = 9 * step_a + 3 * step_b
            table = (select * keeping[..., first : first + 3, None]).astype(jnp.bfloat16)
            picked = jnp.einsum(
                "xyscp,xypw->xyscw", table, column, preferred_element_type=jnp.float32
            )
            pieces.append(picked.astype(jnp.bfloat16))
    gathered = jnp.stack(pieces, axis=3)
    gathered = gathered.reshape(gathered.shape[:3] + (27, gathered.shape[-1]))
    return jnp.einsum("xysoj,xysoij->xysi", gathered, matrix, preferred_element_type=jnp.float32)


def by_plane(vector, order):
    places = jnp.arange(order.shape[2], dtype=jnp.int32)
    table = (order[..., None] == places).astype(jnp.bfloat16)
    moved = jnp.einsum("xysp,xysw->xypw", table, vector, preferred_element_type=jnp.float32)
    return moved.astype(jnp.bfloat16)


def local(blocks, pattern, order, start, rhs):
    depth = blocks.shape[2]
    first = lax.axis_index("gz") * depth
    smoothed, target = (start, rhs)
    rows = lax.dynamic_slice_in_dim(order, first, depth, 2)
    present = lax.dynamic_slice_in_dim(pattern, first, depth, 2)

    def operator(vector):
        column = lax.all_gather(vector.astype(jnp.bfloat16), "gz", axis=2, tiled=True)
        planes = by_plane(column, order)
        return coupled_product(blocks, planes, rows, present)

    center = 1.0
    spread = 0.8
    sigma = center / spread
    rho = 1.0 / sigma
    remainder = target - operator(smoothed)
    search = remainder / center
    for number in range(DEG):
        smoothed = smoothed + search
        remainder = remainder - operator(search)
        if number + 1 < DEG:
            following = 1.0 / (2.0 * sigma - rho)
            search = following * rho * search + 2.0 * following / spread * remainder
            rho = following
    return (smoothed, remainder)


def solution(mesh):
    in_specs = (
        P("gx", "gy", "gz", None, None, None),
        P("gx", "gy", None, None),
        P("gx", "gy", None),
        P("gx", "gy", "gz", None),
        P("gx", "gy", "gz", None),
    )
    out_specs = (P("gx", "gy", "gz", None), P("gx", "gy", "gz", None))
    return jax.shard_map(local, mesh=mesh, in_specs=in_specs, out_specs=out_specs, check_vma=False)
```

profile of v0, /device:TPU:97, one launch (start us, length us, event | category | flops | bytes accessed | tf_op | source)
XLA Modules:
  0.0 160.3 jit_solution(5242034563477572541)
XLA Ops:
  1.5 7.8 %all_gather.15 = bf16[2,1,8,128]{3,0,1,2:T(2,128)(2,1)S(1)} all-gather(bf16[2,1,2,128]{3,0,1,2:T(2,128)(2,1)S(1)} %copy.155), channel_id=1, replica_groups=mesh['gx'=8,'gy'=8,'gz'=4] {'gz'}, dimensions={2}, use_global_device_ids=true | all-gather | bytes 5120 | tf_op jit(solution)/shard_map/all_gather | solution.py:66
  10.7 7.8 %collective-permute-start = (bf16[1,1,8,128]{3,2,0,1:T(8,128)(2,1)}, bf16[1,1,8,128]{3,2,0,1:T(8,128)(2,1)S(1)}, u32[]{:S(2)}, u32[]{:S(2)}) collective-permute-start(bf16[1,1,8,128]{3,2,0,1:T(8,128)(2,1)} %get-tuple-element.24), channel_id=1, source_target_pairs={{0,32},{32,64},{64,96},{96,128},{128,160},{160,192},{192,224},{1,3... | collective-permute-start | bytes 6152 | tf_op jit(solution)/shard_map/ppermute | solution.py:17
  18.5 1.9 %collective-permute-start.1 = (bf16[1,1,8,128]{3,2,1,0:T(8,128)(2,1)}, bf16[1,1,8,128]{3,2,1,0:T(8,128)(2,1)S(1)}, u32[]{:S(2)}, u32[]{:S(2)}) collective-permute-start(bf16[1,1,8,128]{3,2,1,0:T(8,128)(2,1)} %get-tuple-element.25), channel_id=1, source_target_pairs={{32,0},{64,32},{96,64},{128,96},{160,128},{192,160},{224,192},{33,... | collective-permute-start | bytes 6152 | tf_op jit(solution)/shard_map/ppermute | solution.py:19
  22.6 3.1 %collective-permute-done.1 = bf16[1,1,8,128]{3,2,1,0:T(8,128)(2,1)S(1)} collective-permute-done((bf16[1,1,8,128]{3,2,1,0:T(8,128)(2,1)}, bf16[1,1,8,128]{3,2,1,0:T(8,128)(2,1)S(1)}, u32[]{:S(2)}, u32[]{:S(2)}) %collective-permute-start.1) | collective-permute-done | bytes 2080 | tf_op jit(solution)/shard_map/ppermute | solution.py:19
  25.7 5.1 %collective-permute-start.3 = (bf16[4,1,8,128]{3,2,0,1:T(8,128)(2,1)S(1)}, bf16[4,1,8,128]{3,2,0,1:T(8,128)(2,1)S(1)}, u32[]{:S(2)}, u32[]{:S(2)}) collective-permute-start(bf16[4,1,8,128]{3,2,0,1:T(8,128)(2,1)S(1)} %pad_maximum_fusion), channel_id=1, source_target_pairs={{4,0},{8,4},{12,8},{16,12},{20,16},{24,20},{28,24},{5,1},{9,5},{13... | collective-permute-start | bytes 24584 | tf_op jit(solution)/shard_map/ppermute | solution.py:19
  30.8 1.9 %collective-permute-start.2 = (bf16[4,1,8,128]{3,2,0,1:T(8,128)(2,1)S(1)}, bf16[4,1,8,128]{3,2,0,1:T(8,128)(2,1)S(1)}, u32[]{:S(2)}, u32[]{:S(2)}) collective-permute-start(bf16[4,1,8,128]{3,2,0,1:T(8,128)(2,1)S(1)} %pad_maximum_fusion), channel_id=1, source_target_pairs={{0,4},{4,8},{8,12},{12,16},{16,20},{20,24},{24,28},{1,5},{5,9},{9,... | collective-permute-start | bytes 24584 | tf_op jit(solution)/shard_map/ppermute | solution.py:17
  32.8 4.5 %collective-permute-done.2 = bf16[4,1,8,128]{3,2,0,1:T(8,128)(2,1)S(1)} collective-permute-done((bf16[4,1,8,128]{3,2,0,1:T(8,128)(2,1)S(1)}, bf16[4,1,8,128]{3,2,0,1:T(8,128)(2,1)S(1)}, u32[]{:S(2)}, u32[]{:S(2)}) %collective-permute-start.2) | collective-permute-done | bytes 8224 | tf_op jit(solution)/shard_map/ppermute | solution.py:17
  40.3 5.3 %all_gather.16 = bf16[2,1,8,128]{3,0,1,2:T(2,128)(2,1)S(1)} all-gather(bf16[2,1,2,128]{3,0,1,2:T(2,128)(2,1)S(1)} %get-tuple-element.12), channel_id=1, replica_groups=mesh['gx'=8,'gy'=8,'gz'=4] {'gz'}, dimensions={2}, use_global_device_ids=true | all-gather | bytes 5120 | tf_op jit(solution)/shard_map/all_gather | solution.py:66
  45.7 5.8 %collective-permute-start.4 = (bf16[1,1,8,128]{3,2,0,1:T(8,128)(2,1)S(1)}, bf16[1,1,8,128]{3,2,0,1:T(8,128)(2,1)S(1)}, u32[]{:S(2)}, u32[]{:S(2)}) collective-permute-start(bf16[1,1,8,128]{3,2,0,1:T(8,128)(2,1)S(1)} %get-tuple-element.22), channel_id=1, source_target_pairs={{0,32},{32,64},{64,96},{96,128},{128,160},{160,192},{192,224},{1,3... | collective-permute-start | bytes 6152 | tf_op jit(solution)/shard_map/ppermute | solution.py:17
  51.4 1.9 %collective-permute-start.5 = (bf16[1,1,8,128]{3,2,1,0:T(8,128)(2,1)S(1)}, bf16[1,1,8,128]{3,2,1,0:T(8,128)(2,1)S(1)}, u32[]{:S(2)}, u32[]{:S(2)}) collective-permute-start(bf16[1,1,8,128]{3,2,1,0:T(8,128)(2,1)S(1)} %get-tuple-element.23), channel_id=1, source_target_pairs={{32,0},{64,32},{96,64},{128,96},{160,128},{192,160},{224,192},{33,... | collective-permute-start | bytes 6152 | tf_op jit(solution)/shard_map/ppermute | solution.py:19
  53.4 5.1 %collective-permute-done.5 = bf16[1,1,8,128]{3,2,1,0:T(8,128)(2,1)S(1)} collective-permute-done((bf16[1,1,8,128]{3,2,1,0:T(8,128)(2,1)S(1)}, bf16[1,1,8,128]{3,2,1,0:T(8,128)(2,1)S(1)}, u32[]{:S(2)}, u32[]{:S(2)}) %collective-permute-start.5) | collective-permute-done | bytes 2080 | tf_op jit(solution)/shard_map/ppermute | solution.py:19
  58.5 1.9 %collective-permute-start.7 = (bf16[4,1,8,128]{3,2,0,1:T(8,128)(2,1)S(1)}, bf16[4,1,8,128]{3,2,0,1:T(8,128)(2,1)S(1)}, u32[]{:S(2)}, u32[]{:S(2)}) collective-permute-start(bf16[4,1,8,128]{3,2,0,1:T(8,128)(2,1)S(1)} %pad_maximum_fusion.1), channel_id=1, source_target_pairs={{4,0},{8,4},{12,8},{16,12},{20,16},{24,20},{28,24},{5,1},{9,5},{13... | collective-permute-start | bytes 24584 | tf_op jit(solution)/shard_map/ppermute | solution.py:19
  60.4 3.4 %collective-permute-start.6 = (bf16[4,1,8,128]{3,2,0,1:T(8,128)(2,1)S(1)}, bf16[4,1,8,128]{3,2,0,1:T(8,128)(2,1)S(1)}, u32[]{:S(2)}, u32[]{:S(2)}) collective-permute-start(bf16[4,1,8,128]{3,2,0,1:T(8,128)(2,1)S(1)} %pad_maximum_fusion.1), channel_id=1, source_target_pairs={{0,4},{4,8},{8,12},{12,16},{16,20},{20,24},{24,28},{1,5},{5,9},{9,... | collective-permute-start | bytes 24584 | tf_op jit(solution)/shard_map/ppermute | solution.py:17
  63.8 3.1 %collective-permute-done.6 = bf16[4,1,8,128]{3,2,0,1:T(8,128)(2,1)S(1)} collective-permute-done((bf16[4,1,8,128]{3,2,0,1:T(8,128)(2,1)S(1)}, bf16[4,1,8,128]{3,2,0,1:T(8,128)(2,1)S(1)}, u32[]{:S(2)}, u32[]{:S(2)}) %collective-permute-start.6) | collective-permute-done | bytes 8224 | tf_op jit(solution)/shard_map/ppermute | solution.py:17
  69.8 7.0 %all_gather.17 = bf16[2,1,8,128]{3,0,1,2:T(2,128)(2,1)S(1)} all-gather(bf16[2,1,2,128]{3,0,1,2:T(2,128)(2,1)S(1)} %get-tuple-element.10), channel_id=1, replica_groups=mesh['gx'=8,'gy'=8,'gz'=4] {'gz'}, dimensions={2}, use_global_device_ids=true | all-gather | bytes 5120 | tf_op jit(solution)/shard_map/all_gather | solution.py:66
  76.9 5.1 %collective-permute-start.8 = (bf16[1,1,8,128]{3,2,0,1:T(8,128)(2,1)S(1)}, bf16[1,1,8,128]{3,2,0,1:T(8,128)(2,1)S(1)}, u32[]{:S(2)}, u32[]{:S(2)}) collective-permute-start(bf16[1,1,8,128]{3,2,0,1:T(8,128)(2,1)S(1)} %get-tuple-element.20), channel_id=1, source_target_pairs={{0,32},{32,64},{64,96},{96,128},{128,160},{160,192},{192,224},{1,3... | collective-permute-start | bytes 6152 | tf_op jit(solution)/shard_map/ppermute | solution.py:17
  82.1 1.9 %collective-permute-start.9 = (bf16[1,1,8,128]{3,2,1,0:T(8,128)(2,1)S(1)}, bf16[1,1,8,128]{3,2,1,0:T(8,128)(2,1)S(1)}, u32[]{:S(2)}, u32[]{:S(2)}) collective-permute-start(bf16[1,1,8,128]{3,2,1,0:T(8,128)(2,1)S(1)} %get-tuple-element.21), channel_id=1, source_target_pairs={{32,0},{64,32},{96,64},{128,96},{160,128},{192,160},{224,192},{33,... | collective-permute-start | bytes 6152 | tf_op jit(solution)/shard_map/ppermute | solution.py:19
  84.0 5.1 %collective-permute-done.9 = bf16[1,1,8,128]{3,2,1,0:T(8,128)(2,1)S(1)} collective-permute-done((bf16[1,1,8,128]{3,2,1,0:T(8,128)(2,1)S(1)}, bf16[1,1,8,128]{3,2,1,0:T(8,128)(2,1)S(1)}, u32[]{:S(2)}, u32[]{:S(2)}) %collective-permute-start.9) | collective-permute-done | bytes 2080 | tf_op jit(solution)/shard_map/ppermute | solution.py:19
  91.0 3.4 %collective-permute-start.10 = (bf16[4,1,8,128]{3,2,0,1:T(8,128)(2,1)S(1)}, bf16[4,1,8,128]{3,2,0,1:T(8,128)(2,1)S(1)}, u32[]{:S(2)}, u32[]{:S(2)}) collective-permute-start(bf16[4,1,8,128]{3,2,0,1:T(8,128)(2,1)S(1)} %pad_maximum_fusion.2), channel_id=1, source_target_pairs={{0,4},{4,8},{8,12},{12,16},{16,20},{20,24},{24,28},{1,5},{5,9},{9,... | collective-permute-start | bytes 24584 | tf_op jit(solution)/shard_map/ppermute | solution.py:17
  94.4 3.1 %collective-permute-done.10 = bf16[4,1,8,128]{3,2,0,1:T(8,128)(2,1)S(1)} collective-permute-done((bf16[4,1,8,128]{3,2,0,1:T(8,128)(2,1)S(1)}, bf16[4,1,8,128]{3,2,0,1:T(8,128)(2,1)S(1)}, u32[]{:S(2)}, u32[]{:S(2)}) %collective-permute-start.10) | collective-permute-done | bytes 8224 | tf_op jit(solution)/shard_map/ppermute | solution.py:17
  100.5 5.3 %all_gather.18 = bf16[2,1,8,128]{3,0,1,2:T(2,128)(2,1)S(1)} all-gather(bf16[2,1,2,128]{3,0,1,2:T(2,128)(2,1)S(1)} %get-tuple-element.8), channel_id=1, replica_groups=mesh['gx'=8,'gy'=8,'gz'=4] {'gz'}, dimensions={2}, use_global_device_ids=true | all-gather | bytes 5120 | tf_op jit(solution)/shard_map/all_gather | solution.py:66
  105.8 4.8 %collective-permute-start.12 = (bf16[1,1,8,128]{3,2,0,1:T(8,128)(2,1)S(1)}, bf16[1,1,8,128]{3,2,0,1:T(8,128)(2,1)S(1)}, u32[]{:S(2)}, u32[]{:S(2)}) collective-permute-start(bf16[1,1,8,128]{3,2,0,1:T(8,128)(2,1)S(1)} %get-tuple-element.18), channel_id=1, source_target_pairs={{0,32},{32,64},{64,96},{96,128},{128,160},{160,192},{192,224},{1,3... | collective-permute-start | bytes 6152 | tf_op jit(solution)/shard_map/ppermute | solution.py:17
  110.7 1.9 %collective-permute-start.13 = (bf16[1,1,8,128]{3,2,1,0:T(8,128)(2,1)S(1)}, bf16[1,1,8,128]{3,2,1,0:T(8,128)(2,1)S(1)}, u32[]{:S(2)}, u32[]{:S(2)}) collective-permute-start(bf16[1,1,8,128]{3,2,1,0:T(8,128)(2,1)S(1)} %get-tuple-element.19), channel_id=1, source_target_pairs={{32,0},{64,32},{96,64},{128,96},{160,128},{192,160},{224,192},{33,... | collective-permute-start | bytes 6152 | tf_op jit(solution)/shard_map/ppermute | solution.py:19
  112.6 5.1 %collective-permute-done.13 = bf16[1,1,8,128]{3,2,1,0:T(8,128)(2,1)S(1)} collective-permute-done((bf16[1,1,8,128]{3,2,1,0:T(8,128)(2,1)S(1)}, bf16[1,1,8,128]{3,2,1,0:T(8,128)(2,1)S(1)}, u32[]{:S(2)}, u32[]{:S(2)}) %collective-permute-start.13) | collective-permute-done | bytes 2080 | tf_op jit(solution)/shard_map/ppermute | solution.py:19
  119.6 3.4 %collective-permute-start.14 = (bf16[4,1,8,128]{3,2,0,1:T(8,128)(2,1)S(1)}, bf16[4,1,8,128]{3,2,0,1:T(8,128)(2,1)S(1)}, u32[]{:S(2)}, u32[]{:S(2)}) collective-permute-start(bf16[4,1,8,128]{3,2,0,1:T(8,128)(2,1)S(1)} %pad_maximum_fusion.3), channel_id=1, source_target_pairs={{0,4},{4,8},{8,12},{12,16},{16,20},{20,24},{24,28},{1,5},{5,9},{9,... | collective-permute-start | bytes 24584 | tf_op jit(solution)/shard_map/ppermute | solution.py:17
  123.0 3.1 %collective-permute-done.14 = bf16[4,1,8,128]{3,2,0,1:T(8,128)(2,1)S(1)} collective-permute-done((bf16[4,1,8,128]{3,2,0,1:T(8,128)(2,1)S(1)}, bf16[4,1,8,128]{3,2,0,1:T(8,128)(2,1)S(1)}, u32[]{:S(2)}, u32[]{:S(2)}) %collective-permute-start.14) | collective-permute-done | bytes 8224 | tf_op jit(solution)/shard_map/ppermute | solution.py:17
  129.1 7.0 %all_gather.19 = bf16[2,1,8,128]{3,0,1,2:T(2,128)(2,1)S(1)} all-gather(bf16[2,1,2,128]{3,0,1,2:T(2,128)(2,1)S(1)} %get-tuple-element.14), channel_id=1, replica_groups=mesh['gx'=8,'gy'=8,'gz'=4] {'gz'}, dimensions={2}, use_global_device_ids=true | all-gather | bytes 5120 | tf_op jit(solution)/shard_map/all_gather | solution.py:66
  136.2 5.1 %collective-permute-start.16 = (bf16[1,1,8,128]{3,2,0,1:T(8,128)(2,1)S(1)}, bf16[1,1,8,128]{3,2,0,1:T(8,128)(2,1)S(1)}, u32[]{:S(2)}, u32[]{:S(2)}) collective-permute-start(bf16[1,1,8,128]{3,2,0,1:T(8,128)(2,1)S(1)} %get-tuple-element.16), channel_id=1, source_target_pairs={{0,32},{32,64},{64,96},{96,128},{128,160},{160,192},{192,224},{1,3... | collective-permute-start | bytes 6152 | tf_op jit(solution)/shard_map/ppermute | solution.py:17
  141.3 1.9 %collective-permute-start.17 = (bf16[1,1,8,128]{3,2,1,0:T(8,128)(2,1)S(1)}, bf16[1,1,8,128]{3,2,1,0:T(8,128)(2,1)S(1)}, u32[]{:S(2)}, u32[]{:S(2)}) collective-permute-start(bf16[1,1,8,128]{3,2,1,0:T(8,128)(2,1)S(1)} %get-tuple-element.17), channel_id=1, source_target_pairs={{32,0},{64,32},{96,64},{128,96},{160,128},{192,160},{224,192},{33,... | collective-permute-start | bytes 6152 | tf_op jit(solution)/shard_map/ppermute | solution.py:19
  143.2 5.1 %collective-permute-done.17 = bf16[1,1,8,128]{3,2,1,0:T(8,128)(2,1)S(1)} collective-permute-done((bf16[1,1,8,128]{3,2,1,0:T(8,128)(2,1)S(1)}, bf16[1,1,8,128]{3,2,1,0:T(8,128)(2,1)S(1)}, u32[]{:S(2)}, u32[]{:S(2)}) %collective-permute-start.17) | collective-permute-done | bytes 2080 | tf_op jit(solution)/shard_map/ppermute | solution.py:19
  150.2 3.4 %collective-permute-start.18 = (bf16[4,1,8,128]{3,2,0,1:T(8,128)(2,1)S(1)}, bf16[4,1,8,128]{3,2,0,1:T(8,128)(2,1)S(1)}, u32[]{:S(2)}, u32[]{:S(2)}) collective-permute-start(bf16[4,1,8,128]{3,2,0,1:T(8,128)(2,1)S(1)} %pad_maximum_fusion.4), channel_id=1, source_target_pairs={{0,4},{4,8},{8,12},{12,16},{16,20},{20,24},{24,28},{1,5},{5,9},{9,... | collective-permute-start | bytes 24584 | tf_op jit(solution)/shard_map/ppermute | solution.py:17
  154.2 2.6 %collective-permute-done.18 = bf16[4,1,8,128]{3,2,0,1:T(8,128)(2,1)S(1)} collective-permute-done((bf16[4,1,8,128]{3,2,0,1:T(8,128)(2,1)S(1)}, bf16[4,1,8,128]{3,2,0,1:T(8,128)(2,1)S(1)}, u32[]{:S(2)}, u32[]{:S(2)}) %collective-permute-start.18) | collective-permute-done | bytes 8224 | tf_op jit(solution)/shard_map/ppermute | solution.py:17
  (109 shorter events, 26.6 us)
Async XLA Ops:
  0.6 38.6 %copy-start = (bf16[2,1,2,27,128,128]{5,4,3,2,1,0:T(8,128)(2,1)S(1)}, bf16[2,1,2,27,128,128]{5,4,3,2,1,0:T(8,128)(2,1)}, u32[]{:S(2)}) copy-start(bf16[2,1,2,27,128,128]{5,4,3,2,1,0:T(8,128)(2,1)} %param.5) | copy-start | bytes 10616836
  0.6 44.9 %copy-start.1 = (s32[2,1,8]{2,1,0:T(1,128)S(1)}, s32[2,1,8]{2,1,0:T(1,128)}, u32[]{:S(2)}) copy-start(s32[2,1,8]{2,1,0:T(1,128)} %param.7) | copy-start | bytes 196
  10.7 11.9 %collective-permute-start = (bf16[1,1,8,128]{3,2,0,1:T(8,128)(2,1)}, bf16[1,1,8,128]{3,2,0,1:T(8,128)(2,1)S(1)}, u32[]{:S(2)}, u32[]{:S(2)}) collective-permute-start(bf16[1,1,8,128]{3,2,0,1:T(8,128)(2,1)} %get-tuple-element.24), channel_id=1, source_target_pairs={{0,32},{32,64},{64,96},{96,128},{128,160},{160,192},{192,224},{1,3... | collective-permute-start | bytes 6152 | tf_op jit(solution)/shard_map/ppermute | solution.py:17
  18.5 7.2 %collective-permute-start.1 = (bf16[1,1,8,128]{3,2,1,0:T(8,128)(2,1)}, bf16[1,1,8,128]{3,2,1,0:T(8,128)(2,1)S(1)}, u32[]{:S(2)}, u32[]{:S(2)}) collective-permute-start(bf16[1,1,8,128]{3,2,1,0:T(8,128)(2,1)} %get-tuple-element.25), channel_id=1, source_target_pairs={{32,0},{64,32},{96,64},{128,96},{160,128},{192,160},{224,192},{33,... | collective-permute-start | bytes 6152 | tf_op jit(solution)/shard_map/ppermute | solution.py:19
  21.0 19.2 %copy-start.3 = (f32[2,1,2,128]{3,2,1,0:T(2,128)S(1)}, f32[2,1,2,128]{3,2,1,0:T(2,128)}, u32[]{:S(2)}) copy-start(f32[2,1,2,128]{3,2,1,0:T(2,128)} %param.9) | copy-start | bytes 6148
  25.7 7.1 %collective-permute-start.3 = (bf16[4,1,8,128]{3,2,0,1:T(8,128)(2,1)S(1)}, bf16[4,1,8,128]{3,2,0,1:T(8,128)(2,1)S(1)}, u32[]{:S(2)}, u32[]{:S(2)}) collective-permute-start(bf16[4,1,8,128]{3,2,0,1:T(8,128)(2,1)S(1)} %pad_maximum_fusion), channel_id=1, source_target_pairs={{4,0},{8,4},{12,8},{16,12},{20,16},{24,20},{28,24},{5,1},{9,5},{13... | collective-permute-start | bytes 24584 | tf_op jit(solution)/shard_map/ppermute | solution.py:19
  30.8 6.5 %collective-permute-start.2 = (bf16[4,1,8,128]{3,2,0,1:T(8,128)(2,1)S(1)}, bf16[4,1,8,128]{3,2,0,1:T(8,128)(2,1)S(1)}, u32[]{:S(2)}, u32[]{:S(2)}) collective-permute-start(bf16[4,1,8,128]{3,2,0,1:T(8,128)(2,1)S(1)} %pad_maximum_fusion), channel_id=1, source_target_pairs={{0,4},{4,8},{8,12},{12,16},{16,20},{20,24},{24,28},{1,5},{5,9},{9,... | collective-permute-start | bytes 24584 | tf_op jit(solution)/shard_map/ppermute | solution.py:17
  45.7 7.7 %collective-permute-start.4 = (bf16[1,1,8,128]{3,2,0,1:T(8,128)(2,1)S(1)}, bf16[1,1,8,128]{3,2,0,1:T(8,128)(2,1)S(1)}, u32[]{:S(2)}, u32[]{:S(2)}) collective-permute-start(bf16[1,1,8,128]{3,2,0,1:T(8,128)(2,1)S(1)} %get-tuple-element.22), channel_id=1, source_target_pairs={{0,32},{32,64},{64,96},{96,128},{128,160},{160,192},{192,224},{1,3... | collective-permute-start | bytes 6152 | tf_op jit(solution)/shard_map/ppermute | solution.py:17
  51.4 7.0 %collective-permute-start.5 = (bf16[1,1,8,128]{3,2,1,0:T(8,128)(2,1)S(1)}, bf16[1,1,8,128]{3,2,1,0:T(8,128)(2,1)S(1)}, u32[]{:S(2)}, u32[]{:S(2)}) collective-permute-start(bf16[1,1,8,128]{3,2,1,0:T(8,128)(2,1)S(1)} %get-tuple-element.23), channel_id=1, source_target_pairs={{32,0},{64,32},{96,64},{128,96},{160,128},{192,160},{224,192},{33,... | collective-permute-start | bytes 6152 | tf_op jit(solution)/shard_map/ppermute | solution.py:19
  58.5 5.3 %collective-permute-start.7 = (bf16[4,1,8,128]{3,2,0,1:T(8,128)(2,1)S(1)}, bf16[4,1,8,128]{3,2,0,1:T(8,128)(2,1)S(1)}, u32[]{:S(2)}, u32[]{:S(2)}) collective-permute-start(bf16[4,1,8,128]{3,2,0,1:T(8,128)(2,1)S(1)} %pad_maximum_fusion.1), channel_id=1, source_target_pairs={{4,0},{8,4},{12,8},{16,12},{20,16},{24,20},{28,24},{5,1},{9,5},{13... | collective-permute-start | bytes 24584 | tf_op jit(solution)/shard_map/ppermute | solution.py:19
  60.4 6.5 %collective-permute-start.6 = (bf16[4,1,8,128]{3,2,0,1:T(8,128)(2,1)S(1)}, bf16[4,1,8,128]{3,2,0,1:T(8,128)(2,1)S(1)}, u32[]{:S(2)}, u32[]{:S(2)}) collective-permute-start(bf16[4,1,8,128]{3,2,0,1:T(8,128)(2,1)S(1)} %pad_maximum_fusion.1), channel_id=1, source_target_pairs={{0,4},{4,8},{8,12},{12,16},{16,20},{20,24},{24,28},{1,5},{5,9},{9,... | collective-permute-start | bytes 24584 | tf_op jit(solution)/shard_map/ppermute | solution.py:17
  76.9 7.0 %collective-permute-start.8 = (bf16[1,1,8,128]{3,2,0,1:T(8,128)(2,1)S(1)}, bf16[1,1,8,128]{3,2,0,1:T(8,128)(2,1)S(1)}, u32[]{:S(2)}, u32[]{:S(2)}) collective-permute-start(bf16[1,1,8,128]{3,2,0,1:T(8,128)(2,1)S(1)} %get-tuple-element.20), channel_id=1, source_target_pairs={{0,32},{32,64},{64,96},{96,128},{128,160},{160,192},{192,224},{1,3... | collective-permute-start | bytes 6152 | tf_op jit(solution)/shard_map/ppermute | solution.py:17
  82.1 7.0 %collective-permute-start.9 = (bf16[1,1,8,128]{3,2,1,0:T(8,128)(2,1)S(1)}, bf16[1,1,8,128]{3,2,1,0:T(8,128)(2,1)S(1)}, u32[]{:S(2)}, u32[]{:S(2)}) collective-permute-start(bf16[1,1,8,128]{3,2,1,0:T(8,128)(2,1)S(1)} %get-tuple-element.21), channel_id=1, source_target_pairs={{32,0},{64,32},{96,64},{128,96},{160,128},{192,160},{224,192},{33,... | collective-permute-start | bytes 6152 | tf_op jit(solution)/shard_map/ppermute | solution.py:19
  89.1 5.3 %collective-permute-start.11 = (bf16[4,1,8,128]{3,2,0,1:T(8,128)(2,1)S(1)}, bf16[4,1,8,128]{3,2,0,1:T(8,128)(2,1)S(1)}, u32[]{:S(2)}, u32[]{:S(2)}) collective-permute-start(bf16[4,1,8,128]{3,2,0,1:T(8,128)(2,1)S(1)} %pad_maximum_fusion.2), channel_id=1, source_target_pairs={{4,0},{8,4},{12,8},{16,12},{20,16},{24,20},{28,24},{5,1},{9,5},{13... | collective-permute-start | bytes 24584 | tf_op jit(solution)/shard_map/ppermute | solution.py:19
  91.0 6.5 %collective-permute-start.10 = (bf16[4,1,8,128]{3,2,0,1:T(8,128)(2,1)S(1)}, bf16[4,1,8,128]{3,2,0,1:T(8,128)(2,1)S(1)}, u32[]{:S(2)}, u32[]{:S(2)}) collective-permute-start(bf16[4,1,8,128]{3,2,0,1:T(8,128)(2,1)S(1)} %pad_maximum_fusion.2), channel_id=1, source_target_pairs={{0,4},{4,8},{8,12},{12,16},{16,20},{20,24},{24,28},{1,5},{5,9},{9,... | collective-permute-start | bytes 24584 | tf_op jit(solution)/shard_map/ppermute | solution.py:17
  100.4 28.6 %copy-start.2 = (f32[2,1,2,128]{3,2,1,0:T(2,128)S(1)}, f32[2,1,2,128]{3,2,1,0:T(2,128)}, u32[]{:S(2)}) copy-start(f32[2,1,2,128]{3,2,1,0:T(2,128)} %param.8) | copy-start | bytes 6148
  105.8 6.8 %collective-permute-start.12 = (bf16[1,1,8,128]{3,2,0,1:T(8,128)(2,1)S(1)}, bf16[1,1,8,128]{3,2,0,1:T(8,128)(2,1)S(1)}, u32[]{:S(2)}, u32[]{:S(2)}) collective-permute-start(bf16[1,1,8,128]{3,2,0,1:T(8,128)(2,1)S(1)} %get-tuple-element.18), channel_id=1, source_target_pairs={{0,32},{32,64},{64,96},{96,128},{128,160},{160,192},{192,224},{1,3... | collective-permute-start | bytes 6152 | tf_op jit(solution)/shard_map/ppermute | solution.py:17
  110.7 7.0 %collective-permute-start.13 = (bf16[1,1,8,128]{3,2,1,0:T(8,128)(2,1)S(1)}, bf16[1,1,8,128]{3,2,1,0:T(8,128)(2,1)S(1)}, u32[]{:S(2)}, u32[]{:S(2)}) collective-permute-start(bf16[1,1,8,128]{3,2,1,0:T(8,128)(2,1)S(1)} %get-tuple-element.19), channel_id=1, source_target_pairs={{32,0},{64,32},{96,64},{128,96},{160,128},{192,160},{224,192},{33,... | collective-permute-start | bytes 6152 | tf_op jit(solution)/shard_map/ppermute | solution.py:19
  117.7 5.3 %collective-permute-start.15 = (bf16[4,1,8,128]{3,2,0,1:T(8,128)(2,1)S(1)}, bf16[4,1,8,128]{3,2,0,1:T(8,128)(2,1)S(1)}, u32[]{:S(2)}, u32[]{:S(2)}) collective-permute-start(bf16[4,1,8,128]{3,2,0,1:T(8,128)(2,1)S(1)} %pad_maximum_fusion.3), channel_id=1, source_target_pairs={{4,0},{8,4},{12,8},{16,12},{20,16},{24,20},{28,24},{5,1},{9,5},{13... | collective-permute-start | bytes 24584 | tf_op jit(solution)/shard_map/ppermute | solution.py:19
  119.6 6.5 %collective-permute-start.14 = (bf16[4,1,8,128]{3,2,0,1:T(8,128)(2,1)S(1)}, bf16[4,1,8,128]{3,2,0,1:T(8,128)(2,1)S(1)}, u32[]{:S(2)}, u32[]{:S(2)}) collective-permute-start(bf16[4,1,8,128]{3,2,0,1:T(8,128)(2,1)S(1)} %pad_maximum_fusion.3), channel_id=1, source_target_pairs={{0,4},{4,8},{8,12},{12,16},{16,20},{20,24},{24,28},{1,5},{5,9},{9,... | collective-permute-start | bytes 24584 | tf_op jit(solution)/shard_map/ppermute | solution.py:17
  136.2 7.0 %collective-permute-start.16 = (bf16[1,1,8,128]{3,2,0,1:T(8,128)(2,1)S(1)}, bf16[1,1,8,128]{3,2,0,1:T(8,128)(2,1)S(1)}, u32[]{:S(2)}, u32[]{:S(2)}) collective-permute-start(bf16[1,1,8,128]{3,2,0,1:T(8,128)(2,1)S(1)} %get-tuple-element.16), channel_id=1, source_target_pairs={{0,32},{32,64},{64,96},{96,128},{128,160},{160,192},{192,224},{1,3... | collective-permute-start | bytes 6152 | tf_op jit(solution)/shard_map/ppermute | solution.py:17
  141.3 7.0 %collective-permute-start.17 = (bf16[1,1,8,128]{3,2,1,0:T(8,128)(2,1)S(1)}, bf16[1,1,8,128]{3,2,1,0:T(8,128)(2,1)S(1)}, u32[]{:S(2)}, u32[]{:S(2)}) collective-permute-start(bf16[1,1,8,128]{3,2,1,0:T(8,128)(2,1)S(1)} %get-tuple-element.17), channel_id=1, source_target_pairs={{32,0},{64,32},{96,64},{128,96},{160,128},{192,160},{224,192},{33,... | collective-permute-start | bytes 6152 | tf_op jit(solution)/shard_map/ppermute | solution.py:19
  148.3 5.9 %collective-permute-start.19 = (bf16[4,1,8,128]{3,2,0,1:T(8,128)(2,1)S(1)}, bf16[4,1,8,128]{3,2,0,1:T(8,128)(2,1)S(1)}, u32[]{:S(2)}, u32[]{:S(2)}) collective-permute-start(bf16[4,1,8,128]{3,2,0,1:T(8,128)(2,1)S(1)} %pad_maximum_fusion.4), channel_id=1, source_target_pairs={{4,0},{8,4},{12,8},{16,12},{20,16},{24,20},{28,24},{5,1},{9,5},{13... | collective-permute-start | bytes 24584 | tf_op jit(solution)/shard_map/ppermute | solution.py:19
  150.2 6.5 %collective-permute-start.18 = (bf16[4,1,8,128]{3,2,0,1:T(8,128)(2,1)S(1)}, bf16[4,1,8,128]{3,2,0,1:T(8,128)(2,1)S(1)}, u32[]{:S(2)}, u32[]{:S(2)}) collective-permute-start(bf16[4,1,8,128]{3,2,0,1:T(8,128)(2,1)S(1)} %pad_maximum_fusion.4), channel_id=1, source_target_pairs={{0,4},{4,8},{8,12},{12,16},{16,20},{20,24},{24,28},{1,5},{5,9},{9,... | collective-permute-start | bytes 24584 | tf_op jit(solution)/shard_map/ppermute | solution.py:17
where the time goes:
time: 161 us; the launch traced here: 160 us
  starting transfers between devices  66.3 us (41%)
  waiting for transfers between devices  39.9 us (25%)
  blocking collectives  32.3 us (20%)
  matrix products  15.5 us (10%)
  local copies, waits for them, and re-layouts  3.64 us (2%)
  other arithmetic  1.62 us (1%)
    ppermute x10, starting transfers between devices, padded_2(): lax.ppermute(tail, axis, [(i, (i + 1) % count) for i in range(ends)])  44 us
    all_gather x5, blocking collectives, operator(): lax.all_gather(vector.astype(jnp.bfloat16), 'gz', axis=2, tiled=True)  32.3 us
    ppermute x10, waiting for transfers between devices, padded_2(): lax.ppermute(head, axis, [((i + 1) % count, i) for i in range(ends)])  23.5 us
    ppermute x10, starting transfers between devices, padded_2(): lax.ppermute(head, axis, [((i + 1) % count, i) for i in range(ends)])  22.3 us
    ppermute x10, waiting for transfers between devices, padded_2(): lax.ppermute(tail, axis, [(i, (i + 1) % count) for i in range(ends)])  16.4 us
    dot_general x45, matrix products, coupled_product(): jnp.einsum('xyscp,xypw->xyscw', table, column, preferred_element_type=jnp...  9.05 us
    dot_general x5, matrix products, coupled_product(): jnp.einsum('xysoj,xysoij->xysi', gathered, matrix, preferred_element_type...  5.22 us
  transfers between devices with their start and end apart: 20, of which 10 were waited for; matrix products, arithmetic and copies ran while one was open for 2% of the time, Pallas kernels for 0%

commit v1 on v0

--- a/solution.py
+++ b/solution.py
@@ -4,6 +4,27 @@
 from jax.sharding import PartitionSpec as P
 
 DEG = 4
+
+
+def ring_gather(shard, axis, dim):
+    count, place, width = (lax.axis_size(axis), lax.axis_index(axis), shard.shape[dim])
+    ahead = [(i, (i + 1) % count) for i in range(count)]
+    behind = [(i, (i - 1) % count) for i in range(count)]
+    result = jnp.zeros((*shard.shape[:dim], count * width, *shard.shape[dim + 1 :]), shard.dtype)
+    result = lax.dynamic_update_slice_in_dim(result, shard, place * width, axis=dim)
+    from_left = from_right = shard
+    halfway = count // 2
+    for step in range(1, halfway + 1):
+        from_left = lax.ppermute(from_left, axis, ahead)
+        result = lax.dynamic_update_slice_in_dim(
+            result, from_left, (place - step) % count * width, axis=dim
+        )
+        if step < count - halfway:
+            from_right = lax.ppermute(from_right, axis, behind)
+            result = lax.dynamic_update_slice_in_dim(
+                result, from_right, (place + step) % count * width, axis=dim
+            )
+    return result
 
 
 def padded_2(cells, sides, width):
@@ -63,7 +84,7 @@
     present = lax.dynamic_slice_in_dim(pattern, first, depth, 2)
 
     def operator(vector):
-        column = lax.all_gather(vector.astype(jnp.bfloat16), "gz", axis=2, tiled=True)
+        column = ring_gather(vector.astype(jnp.bfloat16), "gz", 2)
         planes = by_plane(column, order)
         return coupled_product(blocks, planes, rows, present)
 

time: 161 us -> 167 us (1.037); the launches traced: 160 us -> 164 us
  starting transfers between devices: 66.3 us -> 108 us
  blocking collectives: 32.3 us -> 0 us
  waiting for transfers between devices: 39.9 us -> 27.2 us
  matrix products: 15.5 us -> 20.9 us
    all_gather x5 -> x0, blocking collectives: 32.3 us -> none  [operator(): lax.all_gather(vector.astype(jnp.bfloat16), 'gz', axis=2, tiled=True)]
    ppermute x10, starting transfers between devices: 22.3 us -> 45.5 us  [padded_2(): lax.ppermute(head, axis, [((i + 1) % count, i) for i in range(ends)])]
    ppermute x0 -> x15, waiting for transfers between devices: none -> 20.6 us  [the longest x10 20.6 us: ring_gather(): from_left = lax.ppermute(from_left, axis, ahead)]
    ppermute x10, waiting for transfers between devices: 23.5 us -> 3.75 us  [padded_2(): lax.ppermute(head, axis, [((i + 1) % count, i) for i in range(ends)])]
    ppermute x0 -> x15, starting transfers between devices: none -> 13.8 us  [the longest x5 12.1 us: ring_gather(): from_right = lax.ppermute(from_right, axis, behind)]
    ppermute x10, waiting for transfers between devices: 16.4 us -> 2.83 us  [padded_2(): lax.ppermute(tail, axis, [(i, (i + 1) % count) for i in range(ends)])]
    dot_general x45, matrix products: 9.05 us -> 14.4 us  [coupled_product(): jnp.einsum('xyscp,xypw->xyscw', table, column, preferred_element_type=jnp...]
    ppermute x10, starting transfers between devices: 44 us -> 49.2 us  [padded_2(): lax.ppermute(tail, axis, [(i, (i + 1) % count) for i in range(ends)])]
  transfers between devices with their start and end apart: 20 -> 35, of which waited for: 10 -> 18; matrix products, arithmetic and copies ran while one was open for 2% -> 2% of each run, Pallas kernels for 0% -> 0%
where the time goes in v1:
time: 167 us; the launch traced here: 164 us
  starting transfers between devices  108 us (65%)
  waiting for transfers between devices  27.2 us (16%)
  matrix products  20.9 us (13%)
  local copies, waits for them, and re-layouts  3.18 us (2%)
  other arithmetic  3.08 us (2%)
    ppermute x10, starting transfers between devices, padded_2(): lax.ppermute(tail, axis, [(i, (i + 1) % count) for i in range(ends)])  49.2 us
    ppermute x10, starting transfers between devices, padded_2(): lax.ppermute(head, axis, [((i + 1) % count, i) for i in range(ends)])  45.5 us
    ppermute x10, waiting for transfers between devices, ring_gather(): from_left = lax.ppermute(from_left, axis, ahead)  20.6 us
    dot_general x45, matrix products, coupled_product(): jnp.einsum('xyscp,xypw->xyscw', table, column, preferred_element_type=jnp...  14.4 us
    ppermute x5, starting transfers between devices, ring_gather(): from_right = lax.ppermute(from_right, axis, behind)  12.1 us
    dot_general x5, matrix products, coupled_product(): jnp.einsum('xysoj,xysoij->xysi', gathered, matrix, preferred_element_type...  5.22 us
    ppermute x10, waiting for transfers between devices, padded_2(): lax.ppermute(head, axis, [((i + 1) % count, i) for i in range(ends)])  3.75 us
  transfers between devices with their start and end apart: 35, of which 18 were waited for; matrix products, arithmetic and copies ran while one was open for 2% of the time, Pallas kernels for 0%

profile of v1, /device:TPU:97, one launch (start us, length us, event | category | flops | bytes accessed | tf_op | source)
XLA Modules:
  0.0 163.9 jit_solution(2815850605844230179)
XLA Ops:
  0.7 1.4 constant_dynamic-update-slice_fusion.19
  2.1 1.2 collective-permute-start
  3.3 1.5 collective-permute-start.1
  7.6 2.3 %collective-permute-done.2 = bf16[2,1,2,128]{3,2,1,0:T(2,128)(2,1)S(1)} collective-permute-done((bf16[2,1,2,128]{3,2,1,0:T(2,128)(2,1)}, bf16[2,1,2,128]{3,2,1,0:T(2,128)(2,1)S(1)}, u32[]{:S(2)}, u32[]{:S(2)}) %collective-permute-start.2) | collective-permute-done | bytes 1056 | tf_op jit(solution)/shard_map/ppermute | solution.py:18
  10.8 4.8 %collective-permute-start.4 = (bf16[1,1,8,128]{3,2,1,0:T(8,128)(2,1)S(1)}, bf16[1,1,8,128]{3,2,1,0:T(8,128)(2,1)S(1)}, u32[]{:S(2)}, u32[]{:S(2)}) collective-permute-start(bf16[1,1,8,128]{3,2,1,0:T(8,128)(2,1)S(1)} %get-tuple-element.26), channel_id=1, source_target_pairs={{32,0},{64,32},{96,64},{128,96},{160,128},{192,160},{224,192},{33,... | collective-permute-start | bytes 6152 | tf_op jit(solution)/shard_map/ppermute | solution.py:40
  15.6 5.1 %collective-permute-start.3 = (bf16[1,1,8,128]{3,2,0,1:T(8,128)(2,1)S(1)}, bf16[1,1,8,128]{3,2,0,1:T(8,128)(2,1)S(1)}, u32[]{:S(2)}, u32[]{:S(2)}) collective-permute-start(bf16[1,1,8,128]{3,2,0,1:T(8,128)(2,1)S(1)} %get-tuple-element.25), channel_id=1, source_target_pairs={{0,32},{32,64},{64,96},{96,128},{128,160},{160,192},{192,224},{1,3... | collective-permute-start | bytes 6152 | tf_op jit(solution)/shard_map/ppermute | solution.py:38
  21.5 3.2 %collective-permute-start.5 = (bf16[4,1,8,128]{3,2,0,1:T(8,128)(2,1)S(1)}, bf16[4,1,8,128]{3,2,0,1:T(8,128)(2,1)S(1)}, u32[]{:S(2)}, u32[]{:S(2)}) collective-permute-start(bf16[4,1,8,128]{3,2,0,1:T(8,128)(2,1)S(1)} %pad_maximum_fusion), channel_id=1, source_target_pairs={{0,4},{4,8},{8,12},{12,16},{16,20},{20,24},{24,28},{1,5},{5,9},{9,... | collective-permute-start | bytes 24584 | tf_op jit(solution)/shard_map/ppermute | solution.py:38
  24.7 4.2 %collective-permute-start.6 = (bf16[4,1,8,128]{3,2,0,1:T(8,128)(2,1)S(1)}, bf16[4,1,8,128]{3,2,0,1:T(8,128)(2,1)S(1)}, u32[]{:S(2)}, u32[]{:S(2)}) collective-permute-start(bf16[4,1,8,128]{3,2,0,1:T(8,128)(2,1)S(1)} %pad_maximum_fusion), channel_id=1, source_target_pairs={{4,0},{8,4},{12,8},{16,12},{20,16},{24,20},{28,24},{5,1},{9,5},{13... | collective-permute-start | bytes 24584 | tf_op jit(solution)/shard_map/ppermute | solution.py:40
  38.1 2.7 %collective-permute-start.8 = (bf16[2,1,2,128]{3,2,1,0:T(2,128)(2,1)S(1)}, bf16[2,1,2,128]{3,2,1,0:T(2,128)(2,1)S(1)}, u32[]{:S(2)}, u32[]{:S(2)}) collective-permute-start(bf16[2,1,2,128]{3,2,1,0:T(2,128)(2,1)S(1)} %get-tuple-element.13), channel_id=1, source_target_pairs={{0,3},{1,0},{2,1},{3,2},{4,7},{5,4},{6,5},{7,6},{8,11},{9,8},{10,9... | collective-permute-start | bytes 3080 | tf_op jit(solution)/shard_map/ppermute | solution.py:23
  41.7 3.6 %collective-permute-done.9 = bf16[2,1,2,128]{3,2,1,0:T(2,128)(2,1)S(1)} collective-permute-done((bf16[2,1,2,128]{3,2,1,0:T(2,128)(2,1)S(1)}, bf16[2,1,2,128]{3,2,1,0:T(2,128)(2,1)S(1)}, u32[]{:S(2)}, u32[]{:S(2)}) %collective-permute-start.9) | collective-permute-done | bytes 1056 | tf_op jit(solution)/shard_map/ppermute | solution.py:18
  45.5 5.2 %collective-permute-start.11 = (bf16[1,1,8,128]{3,2,1,0:T(8,128)(2,1)S(1)}, bf16[1,1,8,128]{3,2,1,0:T(8,128)(2,1)S(1)}, u32[]{:S(2)}, u32[]{:S(2)}) collective-permute-start(bf16[1,1,8,128]{3,2,1,0:T(8,128)(2,1)S(1)} %get-tuple-element.24), channel_id=1, source_target_pairs={{32,0},{64,32},{96,64},{128,96},{160,128},{192,160},{224,192},{33,... | collective-permute-start | bytes 6152 | tf_op jit(solution)/shard_map/ppermute | solution.py:40
  50.7 6.3 %collective-permute-start.10 = (bf16[1,1,8,128]{3,2,0,1:T(8,128)(2,1)S(1)}, bf16[1,1,8,128]{3,2,0,1:T(8,128)(2,1)S(1)}, u32[]{:S(2)}, u32[]{:S(2)}) collective-permute-start(bf16[1,1,8,128]{3,2,0,1:T(8,128)(2,1)S(1)} %get-tuple-element.23), channel_id=1, source_target_pairs={{0,32},{32,64},{64,96},{96,128},{128,160},{160,192},{192,224},{1,3... | collective-permute-start | bytes 6152 | tf_op jit(solution)/shard_map/ppermute | solution.py:38
  57.8 2.9 %collective-permute-start.12 = (bf16[4,1,8,128]{3,2,0,1:T(8,128)(2,1)S(1)}, bf16[4,1,8,128]{3,2,0,1:T(8,128)(2,1)S(1)}, u32[]{:S(2)}, u32[]{:S(2)}) collective-permute-start(bf16[4,1,8,128]{3,2,0,1:T(8,128)(2,1)S(1)} %pad_maximum_fusion.1), channel_id=1, source_target_pairs={{0,4},{4,8},{8,12},{12,16},{16,20},{20,24},{24,28},{1,5},{5,9},{9,... | collective-permute-start | bytes 24584 | tf_op jit(solution)/shard_map/ppermute | solution.py:38
  60.7 5.0 %collective-permute-start.13 = (bf16[4,1,8,128]{3,2,0,1:T(8,128)(2,1)S(1)}, bf16[4,1,8,128]{3,2,0,1:T(8,128)(2,1)S(1)}, u32[]{:S(2)}, u32[]{:S(2)}) collective-permute-start(bf16[4,1,8,128]{3,2,0,1:T(8,128)(2,1)S(1)} %pad_maximum_fusion.1), channel_id=1, source_target_pairs={{4,0},{8,4},{12,8},{16,12},{20,16},{24,20},{28,24},{5,1},{9,5},{13... | collective-permute-start | bytes 24584 | tf_op jit(solution)/shard_map/ppermute | solution.py:40
  69.6 2.7 %collective-permute-start.15 = (bf16[2,1,2,128]{3,2,1,0:T(2,128)(2,1)S(1)}, bf16[2,1,2,128]{3,2,1,0:T(2,128)(2,1)S(1)}, u32[]{:S(2)}, u32[]{:S(2)}) collective-permute-start(bf16[2,1,2,128]{3,2,1,0:T(2,128)(2,1)S(1)} %get-tuple-element.10), channel_id=1, source_target_pairs={{0,3},{1,0},{2,1},{3,2},{4,7},{5,4},{6,5},{7,6},{8,11},{9,8},{10,9... | collective-permute-start | bytes 3080 | tf_op jit(solution)/shard_map/ppermute | solution.py:23
  73.3 3.6 %collective-permute-done.16 = bf16[2,1,2,128]{3,2,1,0:T(2,128)(2,1)S(1)} collective-permute-done((bf16[2,1,2,128]{3,2,1,0:T(2,128)(2,1)S(1)}, bf16[2,1,2,128]{3,2,1,0:T(2,128)(2,1)S(1)}, u32[]{:S(2)}, u32[]{:S(2)}) %collective-permute-start.16) | collective-permute-done | bytes 1056 | tf_op jit(solution)/shard_map/ppermute | solution.py:18
  77.0 3.8 %collective-permute-start.18 = (bf16[1,1,8,128]{3,2,1,0:T(8,128)(2,1)S(1)}, bf16[1,1,8,128]{3,2,1,0:T(8,128)(2,1)S(1)}, u32[]{:S(2)}, u32[]{:S(2)}) collective-permute-start(bf16[1,1,8,128]{3,2,1,0:T(8,128)(2,1)S(1)} %get-tuple-element.22), channel_id=1, source_target_pairs={{32,0},{64,32},{96,64},{128,96},{160,128},{192,160},{224,192},{33,... | collective-permute-start | bytes 6152 | tf_op jit(solution)/shard_map/ppermute | solution.py:40
  80.8 7.5 %collective-permute-start.17 = (bf16[1,1,8,128]{3,2,0,1:T(8,128)(2,1)S(1)}, bf16[1,1,8,128]{3,2,0,1:T(8,128)(2,1)S(1)}, u32[]{:S(2)}, u32[]{:S(2)}) collective-permute-start(bf16[1,1,8,128]{3,2,0,1:T(8,128)(2,1)S(1)} %get-tuple-element.21), channel_id=1, source_target_pairs={{0,32},{32,64},{64,96},{96,128},{128,160},{160,192},{192,224},{1,3... | collective-permute-start | bytes 6152 | tf_op jit(solution)/shard_map/ppermute | solution.py:38
  89.1 2.1 %collective-permute-start.19 = (bf16[4,1,8,128]{3,2,0,1:T(8,128)(2,1)S(1)}, bf16[4,1,8,128]{3,2,0,1:T(8,128)(2,1)S(1)}, u32[]{:S(2)}, u32[]{:S(2)}) collective-permute-start(bf16[4,1,8,128]{3,2,0,1:T(8,128)(2,1)S(1)} %pad_maximum_fusion.2), channel_id=1, source_target_pairs={{0,4},{4,8},{8,12},{12,16},{16,20},{20,24},{24,28},{1,5},{5,9},{9,... | collective-permute-start | bytes 24584 | tf_op jit(solution)/shard_map/ppermute | solution.py:38
  91.2 5.9 %collective-permute-start.20 = (bf16[4,1,8,128]{3,2,0,1:T(8,128)(2,1)S(1)}, bf16[4,1,8,128]{3,2,0,1:T(8,128)(2,1)S(1)}, u32[]{:S(2)}, u32[]{:S(2)}) collective-permute-start(bf16[4,1,8,128]{3,2,0,1:T(8,128)(2,1)S(1)} %pad_maximum_fusion.2), channel_id=1, source_target_pairs={{4,0},{8,4},{12,8},{16,12},{20,16},{24,20},{28,24},{5,1},{9,5},{13... | collective-permute-start | bytes 24584 | tf_op jit(solution)/shard_map/ppermute | solution.py:40
  100.9 2.7 %collective-permute-start.22 = (bf16[2,1,2,128]{3,2,1,0:T(2,128)(2,1)S(1)}, bf16[2,1,2,128]{3,2,1,0:T(2,128)(2,1)S(1)}, u32[]{:S(2)}, u32[]{:S(2)}) collective-permute-start(bf16[2,1,2,128]{3,2,1,0:T(2,128)(2,1)S(1)} %get-tuple-element.6), channel_id=1, source_target_pairs={{0,3},{1,0},{2,1},{3,2},{4,7},{5,4},{6,5},{7,6},{8,11},{9,8},{10,9... | collective-permute-start | bytes 3080 | tf_op jit(solution)/shard_map/ppermute | solution.py:23
  104.5 3.6 %collective-permute-done.23 = bf16[2,1,2,128]{3,2,1,0:T(2,128)(2,1)S(1)} collective-permute-done((bf16[2,1,2,128]{3,2,1,0:T(2,128)(2,1)S(1)}, bf16[2,1,2,128]{3,2,1,0:T(2,128)(2,1)S(1)}, u32[]{:S(2)}, u32[]{:S(2)}) %collective-permute-start.23) | collective-permute-done | bytes 1056 | tf_op jit(solution)/shard_map/ppermute | solution.py:18
  108.3 2.6 %collective-permute-start.25 = (bf16[1,1,8,128]{3,2,1,0:T(8,128)(2,1)S(1)}, bf16[1,1,8,128]{3,2,1,0:T(8,128)(2,1)S(1)}, u32[]{:S(2)}, u32[]{:S(2)}) collective-permute-start(bf16[1,1,8,128]{3,2,1,0:T(8,128)(2,1)S(1)} %get-tuple-element.20), channel_id=1, source_target_pairs={{32,0},{64,32},{96,64},{128,96},{160,128},{192,160},{224,192},{33,... | collective-permute-start | bytes 6152 | tf_op jit(solution)/shard_map/ppermute | solution.py:40
  110.9 8.7 %collective-permute-start.24 = (bf16[1,1,8,128]{3,2,0,1:T(8,128)(2,1)S(1)}, bf16[1,1,8,128]{3,2,0,1:T(8,128)(2,1)S(1)}, u32[]{:S(2)}, u32[]{:S(2)}) collective-permute-start(bf16[1,1,8,128]{3,2,0,1:T(8,128)(2,1)S(1)} %get-tuple-element.19), channel_id=1, source_target_pairs={{0,32},{32,64},{64,96},{96,128},{128,160},{160,192},{192,224},{1,3... | collective-permute-start | bytes 6152 | tf_op jit(solution)/shard_map/ppermute | solution.py:38
  120.4 1.9 %collective-permute-start.26 = (bf16[4,1,8,128]{3,2,0,1:T(8,128)(2,1)S(1)}, bf16[4,1,8,128]{3,2,0,1:T(8,128)(2,1)S(1)}, u32[]{:S(2)}, u32[]{:S(2)}) collective-permute-start(bf16[4,1,8,128]{3,2,0,1:T(8,128)(2,1)S(1)} %pad_maximum_fusion.3), channel_id=1, source_target_pairs={{0,4},{4,8},{8,12},{12,16},{16,20},{20,24},{24,28},{1,5},{5,9},{9,... | collective-permute-start | bytes 24584 | tf_op jit(solution)/shard_map/ppermute | solution.py:38
  122.3 6.0 %collective-permute-start.27 = (bf16[4,1,8,128]{3,2,0,1:T(8,128)(2,1)S(1)}, bf16[4,1,8,128]{3,2,0,1:T(8,128)(2,1)S(1)}, u32[]{:S(2)}, u32[]{:S(2)}) collective-permute-start(bf16[4,1,8,128]{3,2,0,1:T(8,128)(2,1)S(1)} %pad_maximum_fusion.3), channel_id=1, source_target_pairs={{4,0},{8,4},{12,8},{16,12},{20,16},{24,20},{28,24},{5,1},{9,5},{13... | collective-permute-start | bytes 24584 | tf_op jit(solution)/shard_map/ppermute | solution.py:40
  132.1 2.7 %collective-permute-start.29 = (bf16[2,1,2,128]{3,2,1,0:T(2,128)(2,1)S(1)}, bf16[2,1,2,128]{3,2,1,0:T(2,128)(2,1)S(1)}, u32[]{:S(2)}, u32[]{:S(2)}) collective-permute-start(bf16[2,1,2,128]{3,2,1,0:T(2,128)(2,1)S(1)} %get-tuple-element.3), channel_id=1, source_target_pairs={{0,3},{1,0},{2,1},{3,2},{4,7},{5,4},{6,5},{7,6},{8,11},{9,8},{10,9... | collective-permute-start | bytes 3080 | tf_op jit(solution)/shard_map/ppermute | solution.py:23
  135.8 3.6 %collective-permute-done.30 = bf16[2,1,2,128]{3,2,1,0:T(2,128)(2,1)S(1)} collective-permute-done((bf16[2,1,2,128]{3,2,1,0:T(2,128)(2,1)S(1)}, bf16[2,1,2,128]{3,2,1,0:T(2,128)(2,1)S(1)}, u32[]{:S(2)}, u32[]{:S(2)}) %collective-permute-start.30) | collective-permute-done | bytes 1056 | tf_op jit(solution)/shard_map/ppermute | solution.py:18
  139.5 1.9 %collective-permute-start.32 = (bf16[1,1,8,128]{3,2,1,0:T(8,128)(2,1)S(1)}, bf16[1,1,8,128]{3,2,1,0:T(8,128)(2,1)S(1)}, u32[]{:S(2)}, u32[]{:S(2)}) collective-permute-start(bf16[1,1,8,128]{3,2,1,0:T(8,128)(2,1)S(1)} %get-tuple-element.18), channel_id=1, source_target_pairs={{32,0},{64,32},{96,64},{128,96},{160,128},{192,160},{224,192},{33,... | collective-permute-start | bytes 6152 | tf_op jit(solution)/shard_map/ppermute | solution.py:40
  141.4 9.4 %collective-permute-start.31 = (bf16[1,1,8,128]{3,2,0,1:T(8,128)(2,1)S(1)}, bf16[1,1,8,128]{3,2,0,1:T(8,128)(2,1)S(1)}, u32[]{:S(2)}, u32[]{:S(2)}) collective-permute-start(bf16[1,1,8,128]{3,2,0,1:T(8,128)(2,1)S(1)} %get-tuple-element.17), channel_id=1, source_target_pairs={{0,32},{32,64},{64,96},{96,128},{128,160},{160,192},{192,224},{1,3... | collective-permute-start | bytes 6152 | tf_op jit(solution)/shard_map/ppermute | solution.py:38
  151.6 1.9 %collective-permute-start.33 = (bf16[4,1,8,128]{3,2,0,1:T(8,128)(2,1)S(1)}, bf16[4,1,8,128]{3,2,0,1:T(8,128)(2,1)S(1)}, u32[]{:S(2)}, u32[]{:S(2)}) collective-permute-start(bf16[4,1,8,128]{3,2,0,1:T(8,128)(2,1)S(1)} %pad_maximum_fusion.4), channel_id=1, source_target_pairs={{0,4},{4,8},{8,12},{12,16},{16,20},{20,24},{24,28},{1,5},{5,9},{9,... | collective-permute-start | bytes 24584 | tf_op jit(solution)/shard_map/ppermute | solution.py:38
  153.5 6.0 %collective-permute-start.34 = (bf16[4,1,8,128]{3,2,0,1:T(8,128)(2,1)S(1)}, bf16[4,1,8,128]{3,2,0,1:T(8,128)(2,1)S(1)}, u32[]{:S(2)}, u32[]{:S(2)}) collective-permute-start(bf16[4,1,8,128]{3,2,0,1:T(8,128)(2,1)S(1)} %pad_maximum_fusion.4), channel_id=1, source_target_pairs={{4,0},{8,4},{12,8},{16,12},{20,16},{24,20},{28,24},{5,1},{9,5},{13... | collective-permute-start | bytes 24584 | tf_op jit(solution)/shard_map/ppermute | solution.py:40
  (168 shorter events, 36.6 us)
Async XLA Ops:
  2.1 4.1 %collective-permute-start = (bf16[2,1,2,128]{3,2,1,0:T(2,128)(2,1)}, bf16[2,1,2,128]{3,2,1,0:T(2,128)(2,1)}, u32[]{:S(2)}, u32[]{:S(2)}) collective-permute-start(bf16[2,1,2,128]{3,2,1,0:T(2,128)(2,1)} %get-tuple-element.16), channel_id=1, source_target_pairs={{0,1},{1,2},{2,3},{3,0},{4,5},{5,6},{6,7},{7,4},{8,9},{9,10},{10,1... | collective-permute-start | bytes 3080 | tf_op jit(solution)/shard_map/ppermute | solution.py:18
  3.3 3.7 %collective-permute-start.1 = (bf16[2,1,2,128]{3,2,1,0:T(2,128)(2,1)}, bf16[2,1,2,128]{3,2,1,0:T(2,128)(2,1)}, u32[]{:S(2)}, u32[]{:S(2)}) collective-permute-start(bf16[2,1,2,128]{3,2,1,0:T(2,128)(2,1)} %get-tuple-element.16), channel_id=1, source_target_pairs={{0,3},{1,0},{2,1},{3,2},{4,7},{5,4},{6,5},{7,6},{8,11},{9,8},{10,9... | collective-permute-start | bytes 3080 | tf_op jit(solution)/shard_map/ppermute | solution.py:23
  6.2 3.8 %collective-permute-start.2 = (bf16[2,1,2,128]{3,2,1,0:T(2,128)(2,1)}, bf16[2,1,2,128]{3,2,1,0:T(2,128)(2,1)S(1)}, u32[]{:S(2)}, u32[]{:S(2)}) collective-permute-start(bf16[2,1,2,128]{3,2,1,0:T(2,128)(2,1)} %collective-permute-done), channel_id=1, source_target_pairs={{0,1},{1,2},{2,3},{3,0},{4,5},{5,6},{6,7},{7,4},{8,9},{9,10},{10,1... | collective-permute-start | bytes 3080 | tf_op jit(solution)/shard_map/ppermute | solution.py:18
  10.8 10.7 %collective-permute-start.4 = (bf16[1,1,8,128]{3,2,1,0:T(8,128)(2,1)S(1)}, bf16[1,1,8,128]{3,2,1,0:T(8,128)(2,1)S(1)}, u32[]{:S(2)}, u32[]{:S(2)}) collective-permute-start(bf16[1,1,8,128]{3,2,1,0:T(8,128)(2,1)S(1)} %get-tuple-element.26), channel_id=1, source_target_pairs={{32,0},{64,32},{96,64},{128,96},{160,128},{192,160},{224,192},{33,... | collective-permute-start | bytes 6152 | tf_op jit(solution)/shard_map/ppermute | solution.py:40
  15.6 5.9 %collective-permute-start.3 = (bf16[1,1,8,128]{3,2,0,1:T(8,128)(2,1)S(1)}, bf16[1,1,8,128]{3,2,0,1:T(8,128)(2,1)S(1)}, u32[]{:S(2)}, u32[]{:S(2)}) collective-permute-start(bf16[1,1,8,128]{3,2,0,1:T(8,128)(2,1)S(1)} %get-tuple-element.25), channel_id=1, source_target_pairs={{0,32},{32,64},{64,96},{96,128},{128,160},{160,192},{192,224},{1,3... | collective-permute-start | bytes 6152 | tf_op jit(solution)/shard_map/ppermute | solution.py:38
  21.5 7.5 %collective-permute-start.5 = (bf16[4,1,8,128]{3,2,0,1:T(8,128)(2,1)S(1)}, bf16[4,1,8,128]{3,2,0,1:T(8,128)(2,1)S(1)}, u32[]{:S(2)}, u32[]{:S(2)}) collective-permute-start(bf16[4,1,8,128]{3,2,0,1:T(8,128)(2,1)S(1)} %pad_maximum_fusion), channel_id=1, source_target_pairs={{0,4},{4,8},{8,12},{12,16},{16,20},{20,24},{24,28},{1,5},{5,9},{9,... | collective-permute-start | bytes 24584 | tf_op jit(solution)/shard_map/ppermute | solution.py:38
  24.7 5.0 %collective-permute-start.6 = (bf16[4,1,8,128]{3,2,0,1:T(8,128)(2,1)S(1)}, bf16[4,1,8,128]{3,2,0,1:T(8,128)(2,1)S(1)}, u32[]{:S(2)}, u32[]{:S(2)}) collective-permute-start(bf16[4,1,8,128]{3,2,0,1:T(8,128)(2,1)S(1)} %pad_maximum_fusion), channel_id=1, source_target_pairs={{4,0},{8,4},{12,8},{16,12},{20,16},{24,20},{28,24},{5,1},{9,5},{13... | collective-permute-start | bytes 24584 | tf_op jit(solution)/shard_map/ppermute | solution.py:40
  38.0 3.7 %collective-permute-start.7 = (bf16[2,1,2,128]{3,2,1,0:T(2,128)(2,1)S(1)}, bf16[2,1,2,128]{3,2,1,0:T(2,128)(2,1)S(1)}, u32[]{:S(2)}, u32[]{:S(2)}) collective-permute-start(bf16[2,1,2,128]{3,2,1,0:T(2,128)(2,1)S(1)} %get-tuple-element.13), channel_id=1, source_target_pairs={{0,1},{1,2},{2,3},{3,0},{4,5},{5,6},{6,7},{7,4},{8,9},{9,10},{10,1... | collective-permute-start | bytes 3080 | tf_op jit(solution)/shard_map/ppermute | solution.py:18
  38.1 3.6 %collective-permute-start.8 = (bf16[2,1,2,128]{3,2,1,0:T(2,128)(2,1)S(1)}, bf16[2,1,2,128]{3,2,1,0:T(2,128)(2,1)S(1)}, u32[]{:S(2)}, u32[]{:S(2)}) collective-permute-start(bf16[2,1,2,128]{3,2,1,0:T(2,128)(2,1)S(1)} %get-tuple-element.13), channel_id=1, source_target_pairs={{0,3},{1,0},{2,1},{3,2},{4,7},{5,4},{6,5},{7,6},{8,11},{9,8},{10,9... | collective-permute-start | bytes 3080 | tf_op jit(solution)/shard_map/ppermute | solution.py:23
  45.5 11.6 %collective-permute-start.11 = (bf16[1,1,8,128]{3,2,1,0:T(8,128)(2,1)S(1)}, bf16[1,1,8,128]{3,2,1,0:T(8,128)(2,1)S(1)}, u32[]{:S(2)}, u32[]{:S(2)}) collective-permute-start(bf16[1,1,8,128]{3,2,1,0:T(8,128)(2,1)S(1)} %get-tuple-element.24), channel_id=1, source_target_pairs={{32,0},{64,32},{96,64},{128,96},{160,128},{192,160},{224,192},{33,... | collective-permute-start | bytes 6152 | tf_op jit(solution)/shard_map/ppermute | solution.py:40
  50.7 7.0 %collective-permute-start.10 = (bf16[1,1,8,128]{3,2,0,1:T(8,128)(2,1)S(1)}, bf16[1,1,8,128]{3,2,0,1:T(8,128)(2,1)S(1)}, u32[]{:S(2)}, u32[]{:S(2)}) collective-permute-start(bf16[1,1,8,128]{3,2,0,1:T(8,128)(2,1)S(1)} %get-tuple-element.23), channel_id=1, source_target_pairs={{0,32},{32,64},{64,96},{96,128},{128,160},{160,192},{192,224},{1,3... | collective-permute-start | bytes 6152 | tf_op jit(solution)/shard_map/ppermute | solution.py:38
  57.8 7.9 %collective-permute-start.12 = (bf16[4,1,8,128]{3,2,0,1:T(8,128)(2,1)S(1)}, bf16[4,1,8,128]{3,2,0,1:T(8,128)(2,1)S(1)}, u32[]{:S(2)}, u32[]{:S(2)}) collective-permute-start(bf16[4,1,8,128]{3,2,0,1:T(8,128)(2,1)S(1)} %pad_maximum_fusion.1), channel_id=1, source_target_pairs={{0,4},{4,8},{8,12},{12,16},{16,20},{20,24},{24,28},{1,5},{5,9},{9,... | collective-permute-start | bytes 24584 | tf_op jit(solution)/shard_map/ppermute | solution.py:38
  60.7 5.8 %collective-permute-start.13 = (bf16[4,1,8,128]{3,2,0,1:T(8,128)(2,1)S(1)}, bf16[4,1,8,128]{3,2,0,1:T(8,128)(2,1)S(1)}, u32[]{:S(2)}, u32[]{:S(2)}) collective-permute-start(bf16[4,1,8,128]{3,2,0,1:T(8,128)(2,1)S(1)} %pad_maximum_fusion.1), channel_id=1, source_target_pairs={{4,0},{8,4},{12,8},{16,12},{20,16},{24,20},{28,24},{5,1},{9,5},{13... | collective-permute-start | bytes 24584 | tf_op jit(solution)/shard_map/ppermute | solution.py:40
  69.5 3.7 %collective-permute-start.14 = (bf16[2,1,2,128]{3,2,1,0:T(2,128)(2,1)S(1)}, bf16[2,1,2,128]{3,2,1,0:T(2,128)(2,1)S(1)}, u32[]{:S(2)}, u32[]{:S(2)}) collective-permute-start(bf16[2,1,2,128]{3,2,1,0:T(2,128)(2,1)S(1)} %get-tuple-element.10), channel_id=1, source_target_pairs={{0,1},{1,2},{2,3},{3,0},{4,5},{5,6},{6,7},{7,4},{8,9},{9,10},{10,1... | collective-permute-start | bytes 3080 | tf_op jit(solution)/shard_map/ppermute | solution.py:18
  69.6 3.6 %collective-permute-start.15 = (bf16[2,1,2,128]{3,2,1,0:T(2,128)(2,1)S(1)}, bf16[2,1,2,128]{3,2,1,0:T(2,128)(2,1)S(1)}, u32[]{:S(2)}, u32[]{:S(2)}) collective-permute-start(bf16[2,1,2,128]{3,2,1,0:T(2,128)(2,1)S(1)} %get-tuple-element.10), channel_id=1, source_target_pairs={{0,3},{1,0},{2,1},{3,2},{4,7},{5,4},{6,5},{7,6},{8,11},{9,8},{10,9... | collective-permute-start | bytes 3080 | tf_op jit(solution)/shard_map/ppermute | solution.py:23
  77.0 11.4 %collective-permute-start.18 = (bf16[1,1,8,128]{3,2,1,0:T(8,128)(2,1)S(1)}, bf16[1,1,8,128]{3,2,1,0:T(8,128)(2,1)S(1)}, u32[]{:S(2)}, u32[]{:S(2)}) collective-permute-start(bf16[1,1,8,128]{3,2,1,0:T(8,128)(2,1)S(1)} %get-tuple-element.22), channel_id=1, source_target_pairs={{32,0},{64,32},{96,64},{128,96},{160,128},{192,160},{224,192},{33,... | collective-permute-start | bytes 6152 | tf_op jit(solution)/shard_map/ppermute | solution.py:40
  80.8 8.3 %collective-permute-start.17 = (bf16[1,1,8,128]{3,2,0,1:T(8,128)(2,1)S(1)}, bf16[1,1,8,128]{3,2,0,1:T(8,128)(2,1)S(1)}, u32[]{:S(2)}, u32[]{:S(2)}) collective-permute-start(bf16[1,1,8,128]{3,2,0,1:T(8,128)(2,1)S(1)} %get-tuple-element.21), channel_id=1, source_target_pairs={{0,32},{32,64},{64,96},{96,128},{128,160},{160,192},{192,224},{1,3... | collective-permute-start | bytes 6152 | tf_op jit(solution)/shard_map/ppermute | solution.py:38
  89.1 7.9 %collective-permute-start.19 = (bf16[4,1,8,128]{3,2,0,1:T(8,128)(2,1)S(1)}, bf16[4,1,8,128]{3,2,0,1:T(8,128)(2,1)S(1)}, u32[]{:S(2)}, u32[]{:S(2)}) collective-permute-start(bf16[4,1,8,128]{3,2,0,1:T(8,128)(2,1)S(1)} %pad_maximum_fusion.2), channel_id=1, source_target_pairs={{0,4},{4,8},{8,12},{12,16},{16,20},{20,24},{24,28},{1,5},{5,9},{9,... | collective-permute-start | bytes 24584 | tf_op jit(solution)/shard_map/ppermute | solution.py:38
  91.2 6.6 %collective-permute-start.20 = (bf16[4,1,8,128]{3,2,0,1:T(8,128)(2,1)S(1)}, bf16[4,1,8,128]{3,2,0,1:T(8,128)(2,1)S(1)}, u32[]{:S(2)}, u32[]{:S(2)}) collective-permute-start(bf16[4,1,8,128]{3,2,0,1:T(8,128)(2,1)S(1)} %pad_maximum_fusion.2), channel_id=1, source_target_pairs={{4,0},{8,4},{12,8},{16,12},{20,16},{24,20},{28,24},{5,1},{9,5},{13... | collective-permute-start | bytes 24584 | tf_op jit(solution)/shard_map/ppermute | solution.py:40
  100.8 3.7 %collective-permute-start.21 = (bf16[2,1,2,128]{3,2,1,0:T(2,128)(2,1)S(1)}, bf16[2,1,2,128]{3,2,1,0:T(2,128)(2,1)S(1)}, u32[]{:S(2)}, u32[]{:S(2)}) collective-permute-start(bf16[2,1,2,128]{3,2,1,0:T(2,128)(2,1)S(1)} %get-tuple-element.6), channel_id=1, source_target_pairs={{0,1},{1,2},{2,3},{3,0},{4,5},{5,6},{6,7},{7,4},{8,9},{9,10},{10,1... | collective-permute-start | bytes 3080 | tf_op jit(solution)/shard_map/ppermute | solution.py:18
  100.9 3.6 %collective-permute-start.22 = (bf16[2,1,2,128]{3,2,1,0:T(2,128)(2,1)S(1)}, bf16[2,1,2,128]{3,2,1,0:T(2,128)(2,1)S(1)}, u32[]{:S(2)}, u32[]{:S(2)}) collective-permute-start(bf16[2,1,2,128]{3,2,1,0:T(2,128)(2,1)S(1)} %get-tuple-element.6), channel_id=1, source_target_pairs={{0,3},{1,0},{2,1},{3,2},{4,7},{5,4},{6,5},{7,6},{8,11},{9,8},{10,9... | collective-permute-start | bytes 3080 | tf_op jit(solution)/shard_map/ppermute | solution.py:23
  104.5 3.6 %collective-permute-start.23 = (bf16[2,1,2,128]{3,2,1,0:T(2,128)(2,1)S(1)}, bf16[2,1,2,128]{3,2,1,0:T(2,128)(2,1)S(1)}, u32[]{:S(2)}, u32[]{:S(2)}) collective-permute-start(bf16[2,1,2,128]{3,2,1,0:T(2,128)(2,1)S(1)} %collective-permute-done.21), channel_id=1, source_target_pairs={{0,1},{1,2},{2,3},{3,0},{4,5},{5,6},{6,7},{7,4},{8,9},{9,10},{10,1... | collective-permute-start | bytes 3080 | tf_op jit(solution)/shard_map/ppermute | solution.py:18
  108.3 11.4 %collective-permute-start.25 = (bf16[1,1,8,128]{3,2,1,0:T(8,128)(2,1)S(1)}, bf16[1,1,8,128]{3,2,1,0:T(8,128)(2,1)S(1)}, u32[]{:S(2)}, u32[]{:S(2)}) collective-permute-start(bf16[1,1,8,128]{3,2,1,0:T(8,128)(2,1)S(1)} %get-tuple-element.20), channel_id=1, source_target_pairs={{32,0},{64,32},{96,64},{128,96},{160,128},{192,160},{224,192},{33,... | collective-permute-start | bytes 6152 | tf_op jit(solution)/shard_map/ppermute | solution.py:40
  110.9 9.5 %collective-permute-start.24 = (bf16[1,1,8,128]{3,2,0,1:T(8,128)(2,1)S(1)}, bf16[1,1,8,128]{3,2,0,1:T(8,128)(2,1)S(1)}, u32[]{:S(2)}, u32[]{:S(2)}) collective-permute-start(bf16[1,1,8,128]{3,2,0,1:T(8,128)(2,1)S(1)} %get-tuple-element.19), channel_id=1, source_target_pairs={{0,32},{32,64},{64,96},{96,128},{128,160},{160,192},{192,224},{1,3... | collective-permute-start | bytes 6152 | tf_op jit(solution)/shard_map/ppermute | solution.py:38
  120.4 7.9 %collective-permute-start.26 = (bf16[4,1,8,128]{3,2,0,1:T(8,128)(2,1)S(1)}, bf16[4,1,8,128]{3,2,0,1:T(8,128)(2,1)S(1)}, u32[]{:S(2)}, u32[]{:S(2)}) collective-permute-start(bf16[4,1,8,128]{3,2,0,1:T(8,128)(2,1)S(1)} %pad_maximum_fusion.3), channel_id=1, source_target_pairs={{0,4},{4,8},{8,12},{12,16},{16,20},{20,24},{24,28},{1,5},{5,9},{9,... | collective-permute-start | bytes 24584 | tf_op jit(solution)/shard_map/ppermute | solution.py:38
  122.3 6.8 %collective-permute-start.27 = (bf16[4,1,8,128]{3,2,0,1:T(8,128)(2,1)S(1)}, bf16[4,1,8,128]{3,2,0,1:T(8,128)(2,1)S(1)}, u32[]{:S(2)}, u32[]{:S(2)}) collective-permute-start(bf16[4,1,8,128]{3,2,0,1:T(8,128)(2,1)S(1)} %pad_maximum_fusion.3), channel_id=1, source_target_pairs={{4,0},{8,4},{12,8},{16,12},{20,16},{24,20},{28,24},{5,1},{9,5},{13... | collective-permute-start | bytes 24584 | tf_op jit(solution)/shard_map/ppermute | solution.py:40
  132.0 3.7 %collective-permute-start.28 = (bf16[2,1,2,128]{3,2,1,0:T(2,128)(2,1)S(1)}, bf16[2,1,2,128]{3,2,1,0:T(2,128)(2,1)S(1)}, u32[]{:S(2)}, u32[]{:S(2)}) collective-permute-start(bf16[2,1,2,128]{3,2,1,0:T(2,128)(2,1)S(1)} %get-tuple-element.3), channel_id=1, source_target_pairs={{0,1},{1,2},{2,3},{3,0},{4,5},{5,6},{6,7},{7,4},{8,9},{9,10},{10,1... | collective-permute-start | bytes 3080 | tf_op jit(solution)/shard_map/ppermute | solution.py:18
  132.1 3.6 %collective-permute-start.29 = (bf16[2,1,2,128]{3,2,1,0:T(2,128)(2,1)S(1)}, bf16[2,1,2,128]{3,2,1,0:T(2,128)(2,1)S(1)}, u32[]{:S(2)}, u32[]{:S(2)}) collective-permute-start(bf16[2,1,2,128]{3,2,1,0:T(2,128)(2,1)S(1)} %get-tuple-element.3), channel_id=1, source_target_pairs={{0,3},{1,0},{2,1},{3,2},{4,7},{5,4},{6,5},{7,6},{8,11},{9,8},{10,9... | collective-permute-start | bytes 3080 | tf_op jit(solution)/shard_map/ppermute | solution.py:23
  139.5 11.4 %collective-permute-start.32 = (bf16[1,1,8,128]{3,2,1,0:T(8,128)(2,1)S(1)}, bf16[1,1,8,128]{3,2,1,0:T(8,128)(2,1)S(1)}, u32[]{:S(2)}, u32[]{:S(2)}) collective-permute-start(bf16[1,1,8,128]{3,2,1,0:T(8,128)(2,1)S(1)} %get-tuple-element.18), channel_id=1, source_target_pairs={{32,0},{64,32},{96,64},{128,96},{160,128},{192,160},{224,192},{33,... | collective-permute-start | bytes 6152 | tf_op jit(solution)/shard_map/ppermute | solution.py:40
  141.4 10.2 %collective-permute-start.31 = (bf16[1,1,8,128]{3,2,0,1:T(8,128)(2,1)S(1)}, bf16[1,1,8,128]{3,2,0,1:T(8,128)(2,1)S(1)}, u32[]{:S(2)}, u32[]{:S(2)}) collective-permute-start(bf16[1,1,8,128]{3,2,0,1:T(8,128)(2,1)S(1)} %get-tuple-element.17), channel_id=1, source_target_pairs={{0,32},{32,64},{64,96},{96,128},{128,160},{160,192},{192,224},{1,3... | collective-permute-start | bytes 6152 | tf_op jit(solution)/shard_map/ppermute | solution.py:38
  151.6 7.9 %collective-permute-start.33 = (bf16[4,1,8,128]{3,2,0,1:T(8,128)(2,1)S(1)}, bf16[4,1,8,128]{3,2,0,1:T(8,128)(2,1)S(1)}, u32[]{:S(2)}, u32[]{:S(2)}) collective-permute-start(bf16[4,1,8,128]{3,2,0,1:T(8,128)(2,1)S(1)} %pad_maximum_fusion.4), channel_id=1, source_target_pairs={{0,4},{4,8},{8,12},{12,16},{16,20},{20,24},{24,28},{1,5},{5,9},{9,... | collective-permute-start | bytes 24584 | tf_op jit(solution)/shard_map/ppermute | solution.py:38
  153.5 6.8 %collective-permute-start.34 = (bf16[4,1,8,128]{3,2,0,1:T(8,128)(2,1)S(1)}, bf16[4,1,8,128]{3,2,0,1:T(8,128)(2,1)S(1)}, u32[]{:S(2)}, u32[]{:S(2)}) collective-permute-start(bf16[4,1,8,128]{3,2,0,1:T(8,128)(2,1)S(1)} %pad_maximum_fusion.4), channel_id=1, source_target_pairs={{4,0},{8,4},{12,8},{16,12},{20,16},{24,20},{28,24},{5,1},{9,5},{13... | collective-permute-start | bytes 24584 | tf_op jit(solution)/shard_map/ppermute | solution.py:40
  (15 other events, 550.0 us)
